TPU v7x, 32 devices: a whole 2x2x4 slice. The times are simulated.
32 devices in a mesh: grp: 2 (over y), slab: 4 (over z), head: 2 (over x), seq: 2 (over core).
Axes of the slice: x: 2, y: 2, z: 4, core: 2. Of those that a mesh axis runs over, the one named last changes fastest.
Arguments:
- queries: bfloat16 [1024, 5120], P(('grp', 'seq'), 'head'), parts along dimension 0, may hold values from -140 to 140
- query_gain: float32 [5120], P('head'), may hold values from 1.5 to 3
- cache_keys: bfloat16 [4096, 5120], P(('grp', 'slab'), 'head'), parts along dimension 0, may hold values from -120 to 120
- cache_values: bfloat16 [4096, 5120], P(('grp', 'slab'), 'head'), parts along dimension 0, may hold values from -6 to 6
- finished_keys: bfloat16 [1024, 5120], P(('grp', 'slab', 'seq'), 'head'), parts along dimension 0, may hold values from -6 to 6
- finished_values: bfloat16 [1024, 5120], P(('grp', 'slab', 'seq'), 'head'), parts along dimension 0, may hold values from -6 to 6
- new_keys: bfloat16 [1024, 5120], P(('grp', 'slab', 'seq'), 'head'), parts along dimension 0, may hold values from -6 to 6
- new_values: bfloat16 [1024, 5120], P(('grp', 'slab', 'seq'), 'head'), parts along dimension 0, may hold values from -6 to 6
- out_weight: bfloat16 [5120, 5120], P('head', 'slab'), may hold values from -0.25 to 0.25
- time_weight: float32 [256, 5120], P(None, ('slab', 'head')), may hold values from -0.375 to 0.375
- owner: int32 [2], P('grp'), parts along dimension 0, may hold values from 0 to 3
- step: int32 [2], P('grp'), parts along dimension 0, may hold values from 0 to 999
Outputs:
- branch: bfloat16 [1024, 5120], P(('grp', 'seq'), ('slab', 'head')), parts along dimension 0
There are 2 independent parts, one for each index of `grp`. A program takes and returns all parts, laid end to end along the dimension named above; an argument that names none is the same for every part. Nothing has to cross between parts.
All inputs are finite; a program needn't handle non-finite values.
Results may differ from a plain program's by a relative error of at most 0.012.
Values may be sent and summed in bfloat16 or wider, within the bound.
No kernel may reach another device: no remote copies, remote signals or barrier semaphores. Data moves between devices by JAX's collectives and lax.ppermute only.
A program may use at most 64 MiB of HBM per device.

v0:
```python
from functools import reduce
import jax
import jax.numpy as jnp
from jax import lax
from jax.sharding import PartitionSpec as P

HEADS = 40
HD = 128
EPSILON = 1e-06


def local(
    queries,
    query_gain,
    cache_keys,
    cache_values,
    finished_keys,
    finished_values,
    new_keys,
    new_values,
    out_weight,
    time_weight,
    owner,
    step,
):
    row_count = queries.shape[0]
    head_count = queries.shape[1] // HD
    query_float = queries.astype(jnp.float32)
    norm_total = lax.psum(jnp.sum(query_float * query_float, axis=1), "head")
    inverse = lax.rsqrt(norm_total / (HEADS * HD) + EPSILON)
    normed = (
        (query_float * inverse[:, None] * query_gain)
        .astype(jnp.bfloat16)
        .reshape(row_count, head_count, HD)
    )
    is_owner = lax.axis_index("slab") == owner[0]
    whole_keys, whole_values = (
        lax.all_gather(finished_keys, ("slab", "seq"), axis=0, tiled=True),
        lax.all_gather(finished_values, ("slab", "seq"), axis=0, tiled=True),
    )
    fresh_keys, fresh_values = (
        lax.all_gather(new_keys, "seq", axis=0, tiled=True),
        lax.all_gather(new_values, "seq", axis=0, tiled=True),
    )
    key_block = jnp.where(is_owner, whole_keys, cache_keys)
    value_block = jnp.where(is_owner, whole_values, cache_values)
    blocks = [
        (key_block, value_block, jnp.float32(0.0)),
        (fresh_keys, fresh_values, jnp.float32(0.0)),
    ]
    score_scale = 1.0 / HD**0.5
    score_list = []
    for key_block, value_block, penalty in blocks:
        key_heads = key_block.reshape(key_block.shape[0], head_count, HD)
        each_score = jnp.einsum(
            "rhd,khd->hrk", normed, key_heads, preferred_element_type=jnp.float32
        )
        score_list.append(each_score * score_scale)
    row_top = reduce(jnp.maximum, [jnp.max(each_score, axis=2) for each_score in score_list])
    row_mass = jnp.zeros_like(row_top)
    partial_value = jnp.zeros((head_count, row_count, HD), jnp.float32)
    for each_score, (key_block, value_block, penalty) in zip(score_list, blocks):
        raw_weights = jnp.exp(each_score - row_top[:, :, None])
        row_mass = row_mass + jnp.sum(raw_weights, axis=2)
        value_heads = value_block.reshape(value_block.shape[0], head_count, HD)
        partial_value = partial_value + jnp.einsum(
            "hrk,khd->hrd",
            raw_weights.astype(jnp.bfloat16),
            value_heads,
            preferred_element_type=jnp.float32,
        )
    global_top = lax.pmax(row_top, "slab")
    factor = jnp.exp(row_top - global_top)
    sum_share, mass_share = (
        lax.psum_scatter(
            partial_value * factor[:, :, None], "slab", scatter_dimension=1, tiled=True
        ),
        lax.psum_scatter(row_mass * factor, "slab", scatter_dimension=1, tiled=True),
    )
    row_share = (sum_share / mass_share[:, :, None]).astype(jnp.bfloat16)
    attended = lax.all_gather(row_share, "slab", axis=1, tiled=True)
    weight_heads = out_weight.reshape(head_count, HD, out_weight.shape[1])
    projected = jnp.einsum(
        "hrd,hdc->rc", attended, weight_heads, preferred_element_type=jnp.float32
    )
    summed = lax.psum_scatter(projected, "head", scatter_dimension=1, tiled=True)
    half = time_weight.shape[0] // 2
    frequency = jnp.exp(-jnp.log(10000.0) * jnp.arange(half, dtype=jnp.float32) / half)
    phases = step[0].astype(jnp.float32) * frequency
    embedding = jnp.concatenate([jnp.cos(phases), jnp.sin(phases)])
    time_gate = 1.0 + jnp.dot(embedding, time_weight, precision=lax.Precision.HIGHEST)
    return (time_gate * summed).astype(jnp.bfloat16)


def solution(mesh):
    in_specs = (
        P(("grp", "seq"), "head"),
        P("head"),
        P(("grp", "slab"), "head"),
        P(("grp", "slab"), "head"),
        P(("grp", "slab", "seq"), "head"),
        P(("grp", "slab", "seq"), "head"),
        P(("grp", "slab", "seq"), "head"),
        P(("grp", "slab", "seq"), "head"),
        P("head", "slab"),
        P(None, ("slab", "head")),
        P("grp"),
        P("grp"),
    )
    out_specs = P(("grp", "seq"), ("slab", "head"))
    return jax.shard_map(local, mesh=mesh, in_specs=in_specs, out_specs=out_specs, check_vma=False)
```

profile of v0, /device:TPU:0, one launch (start us, length us, event | category | flops | bytes accessed | tf_op | source)
XLA Modules:
  0.0 240.0 jit_solution(8406601955525841598)
XLA Ops:
  8.1 4.5 %copy.36 = bf16[512,2560]{0,1:T(8,128)(2,1)} copy(bf16[512,2560]{1,0:T(8,128)(2,1)} %param.15) | data formatting | bytes 5242880 | tf_op args[3]
  13.9 4.5 %copy.29 = bf16[512,2560]{0,1:T(8,128)(2,1)} copy(bf16[512,2560]{1,0:T(8,128)(2,1)} %param.14) | data formatting | bytes 5242880 | tf_op args[2]
  18.4 2.7 %all_gather.16 = bf16[128,2560]{1,0:T(8,128)(2,1)S(1)} all-gather(bf16[64,2560]{1,0:T(8,128)(2,1)S(1)} %copy-done.4), channel_id=1, replica_groups=mesh['grp'=2,'slab'=4,'head'=2,'seq'=2] {'seq'}, dimensions={0}, use_global_device_ids=true | all-gather | bytes 983040 | tf_op jit(solution)/shard_map/all_gather | solution.py:42
  22.2 2.3 all_gather.18
  25.9 5.5 %psum.7 = f32[256]{0:T(256)S(1)} all-reduce(f32[256]{0:T(256)S(1)} %fusion.6), channel_id=1, replica_groups=mesh['grp'=2,'slab'=4,'head'=2,'seq'=2] {'head'}, use_global_device_ids=true, to_apply=%region_1.0 | all-reduce | flops 256 | bytes 2048 | tf_op jit(solution)/shard_map/psum | solution.py:29
  31.9 1.2 copy-done.1
  33.0 1.7 multiply_reduce_fusion.1
  34.7 10.7 %all-gather.4.cloned.1.call-done = bf16[512,2560]{1,0:T(8,128)(2,1)} async-done(((bf16[64,2560]{1,0:T(8,128)(2,1)}), bf16[512,2560]{1,0:T(8,128)(2,1)}) %all-gather.4.cloned.1.call-update) | async-done | bytes 2621456 | tf_op jit(solution)/shard_map/all_gather | solution.py:38
  45.4 4.4 %copy.28 = bf16[512,2560]{0,1:T(8,128)(2,1)} copy(bf16[512,2560]{1,0:T(8,128)(2,1)} %all-gather.4.cloned.1.call-done) | data formatting | bytes 5242880 | tf_op jit(solution)/shard_map/all_gather | solution.py:38
  49.8 2.1 broadcast_select_fusion.1
  52.0 5.7 %multiply_reduce_fusion = (f32[20,256]{1,0:T(8,128)S(1)}, f32[20,256,512]{2,1,0:T(8,128)}) fusion(bf16[256,20,128]{0,2,1:T(8,128)(2,1)S(1)} %bitcast.25, bf16[512,20,128]{0,2,1:T(8,128)(2,1)S(1)} %bitcast.27), kind=kOutput, calls=%fused_computation.1 | convolution fusion | flops 676326400 | bytes 14438400 | tf_op jit(solution)/shard_map/rhd,khd->hrk/dot_general | solution.py:55
  57.6 18.7 %pmax.7 = f32[20,256]{1,0:T(8,128)S(1)} all-reduce(f32[20,256]{1,0:T(8,128)S(1)} %max.9), channel_id=1, replica_groups=mesh['grp'=2,'slab'=4,'head'=2,'seq'=2] {'slab'}, use_global_device_ids=true, to_apply=%region_4.5 | all-reduce | flops 5120 | bytes 40960 | tf_op jit(solution)/shard_map/pmax | solution.py:72
  76.4 5.9 %fusion = f32[20,256]{1,0:T(8,128)S(1)} fusion(f32[20,256,512]{2,1,0:T(8,128)} %get-tuple-element.8, f32[20,256]{1,0:T(8,128)S(1)} %max.9), kind=kLoop, calls=%fused_computation.2 | loop fusion | flops 7859200 | bytes 10526720 | tf_op jit(solution)/shard_map/reduce_sum | solution.py:64
  82.3 4.4 %copy.35 = bf16[512,2560]{0,1:T(8,128)(2,1)} copy(bf16[512,2560]{1,0:T(8,128)(2,1)} %all-gather.6.cloned.1.call-done) | data formatting | bytes 5242880 | tf_op jit(solution)/shard_map/all_gather | solution.py:39
  86.7 2.0 broadcast_select_fusion
  88.7 7.7 %fusion.2 = f32[20,256,128]{2,1,0:T(8,128)} fusion(bf16[512,20,128]{0,2,1:T(8,128)(2,1)S(1)} %bitcast.26, f32[20,256,512]{2,1,0:T(8,128)} %get-tuple-element.8, f32[20,256]{1,0:T(8,128)S(1)} %max.9), kind=kOutput, calls=%fused_computation.4 | convolution fusion | flops 678952960 | bytes 15749120 | tf_op jit(solution)/shard_map/hrk,khd->hrd/dot_general | solution.py:66
  97.7 4.1 %add_multiply_fusion = f32[20,256,128]{2,1,0:T(8,128)} fusion(f32[20,256,128]{2,1,0:T(8,128)} %fusion.2, bf16[128,20,128]{0,2,1:T(8,128)(2,1)} %bitcast.28, f32[20,256,128]{1,2,0:T(8,128)S(1)} %get-tuple-element.10, f32[20,256]{1,0:T(8,128)S(1)} %get-tuple-element.6, f32[20,256]{1,0:T(8,128)S(1)} %max.9), kind=kOutput, calls=%fused_computation.13 | convolution fusion | flops 171048960 | bytes 8560640 | tf_op jit(solution)/shard_map/hrk,khd->hrd/dot_general | solution.py:66
  101.9 13.7 %reduce-scatter.10.cloned.1.call-done = f32[64,20]{1,0:T(8,128)} async-done(((f32[256,20]{1,0:T(8,128)}), f32[64,20]{1,0:T(8,128)}) %reduce-scatter.10.cloned.1.call-update) | async-done | bytes 5136
  116.4 51.8 %reduce-scatter.6.cloned.1.call-done = f32[20,64,128]{2,1,0:T(8,128)} async-done(((f32[20,256,128]{2,1,0:T(8,128)}), f32[20,64,128]{2,1,0:T(8,128)}) %reduce-scatter.6.cloned.1.call-update) | async-done | bytes 655376 | tf_op jit(solution)/shard_map/reduce_scatter | solution.py:75
  168.2 2.1 divide_convert_fusion
  170.4 32.2 %all-gather.8.cloned.1.call-done = bf16[20,256,128]{2,1,0:T(8,128)(2,1)} async-done(((bf16[20,64,128]{2,1,0:T(8,128)(2,1)}), bf16[20,256,128]{2,1,0:T(8,128)(2,1)}) %all-gather.8.cloned.1.call-update) | async-done | bytes 1310736 | tf_op jit(solution)/shard_map/all_gather | solution.py:81
  202.5 6.2 %convolution_bitcast_fusion = f32[256,1280]{1,0:T(8,128)} fusion(bf16[20,256,128]{2,1,0:T(8,128)(2,1)} %all-gather.8.cloned.1.call-done, bf16[20,128,1280]{2,1,0:T(8,128)(2,1)} %bitcast.33), kind=kOutput, calls=%fused_computation.9 | convolution fusion | flops 1677721600 | bytes 9175040 | tf_op jit(solution)/shard_map/hrd,hdc->rc/dot_general | solution.py:83
  209.9 21.4 %reduce-scatter.8.cloned.1.call-done = f32[256,640]{1,0:T(8,128)} async-done(((f32[256,1280]{1,0:T(8,128)}), f32[256,640]{1,0:T(8,128)}) %reduce-scatter.8.cloned.1.call-update) | async-done | bytes 655376 | tf_op jit(solution)/shard_map/reduce_scatter | solution.py:86
  231.3 1.9 multiply_convert_fusion
  (41 shorter events, 7.9 us)
Async XLA Ops:
  6.5 202.9 %copy-start = (f32[256,640]{1,0:T(8,128)S(1)}, f32[256,640]{1,0:T(8,128)}, u32[]{:S(2)}) copy-start(f32[256,640]{1,0:T(8,128)} %param.21) | copy-start | bytes 1966084
  6.5 38.9 %all-gather.4.cloned.1.call-start = ((), (), s32[]{:S(2)}) async-start(), calls=%async_computation.3 | async-start | bytes 2949120 | tf_op jit(solution)/shard_map/all_gather | solution.py:38
  7.3 75.0 %all-gather.6.cloned.1.call-start = ((), (), s32[]{:S(2)}) async-start(), calls=%async_computation.4 | async-start | bytes 2949120 | tf_op jit(solution)/shard_map/all_gather | solution.py:39
  8.0 107.6 %reduce-scatter.10.cloned.1.call-start = ((), (), s32[]{:S(2)}) async-start(), calls=%async_computation.8 | async-start | bytes 163840
  8.1 5.2 %copy-start.3 = (bf16[256,2560]{1,0:T(8,128)(2,1)S(1)}, bf16[256,2560]{1,0:T(8,128)(2,1)}, u32[]{:S(2)}) copy-start(bf16[256,2560]{1,0:T(8,128)(2,1)} %param.12) | copy-start | bytes 3932164
  13.9 4.5 %copy-start.4 = (bf16[64,2560]{1,0:T(8,128)(2,1)S(1)}, bf16[64,2560]{1,0:T(8,128)(2,1)}, u32[]{:S(2)}) copy-start(bf16[64,2560]{1,0:T(8,128)(2,1)} %param.18) | copy-start | bytes 983044
  13.9 8.3 %copy-start.5 = (bf16[64,2560]{1,0:T(8,128)(2,1)S(1)}, bf16[64,2560]{1,0:T(8,128)(2,1)}, u32[]{:S(2)}) copy-start(bf16[64,2560]{1,0:T(8,128)(2,1)} %param.19) | copy-start | bytes 983044
  21.1 10.4 %copy-start.6 = (f32[2560]{0:T(1024)S(1)}, f32[2560]{0:T(1024)}, u32[]{:S(2)}) copy-start(f32[2560]{0:T(1024)} %param.13) | copy-start | bytes 30724
  31.9 1.2 copy-start.1
  49.8 2.1 copy-start.2
  97.7 70.6 %reduce-scatter.6.cloned.1.call-start = ((), (), s32[]{:S(2)}) async-start(), calls=%async_computation.5 | async-start | bytes 3276800 | tf_op jit(solution)/shard_map/reduce_scatter | solution.py:75
  101.8 100.7 %all-gather.8.cloned.1.call-start = ((), (), s32[]{:S(2)}) async-start(), calls=%async_computation.6 | async-start | bytes 1638400 | tf_op jit(solution)/shard_map/all_gather | solution.py:81
  170.3 61.0 %reduce-scatter.8.cloned.1.call-start = ((), (), s32[]{:S(2)}) async-start(), calls=%async_computation.7 | async-start | bytes 1966080 | tf_op jit(solution)/shard_map/reduce_scatter | solution.py:86
Sparse Core Ops, SparseCore 0:
  9.0 36.4 all-gather.3
  47.1 33.8 all-gather.5
  97.8 17.7 reduce-scatter.9
  117.7 50.4 reduce-scatter.5
  170.4 32.0 all-gather.7
  208.9 22.3 reduce-scatter.7
where the time goes:
time: 241 us; the launch traced here: 240 us
  waiting for transfers between devices  131 us (54%)
  blocking collectives  29.2 us (12%)
  matrix products  25.7 us (11%)
  local copies, waits for them, and re-layouts  23.4 us (10%)
  other arithmetic  15.2 us (6%)
  between operations  14.9 us (6%)
    reduce_scatter x1, waiting for transfers between devices, local(): lax.psum_scatter(partial_value * factor[:, :, None], 'slab', scatter_dime...  51.8 us
    all_gather x1, waiting for transfers between devices, local(): attended = lax.all_gather(row_share, 'slab', axis=1, tiled=True)  32.2 us
    reduce_scatter x1, waiting for transfers between devices, local(): lax.psum_scatter(projected, 'head', scatter_dimension=1, tiled=True)  21.4 us
    pmax x1, blocking collectives, local(): global_top = lax.pmax(row_top, 'slab')  18.7 us
    unnamed x7, waiting for transfers between devices  15.2 us
    unnamed x19, local copies, waits for them, and re-layouts  12.4 us
    dot_general x2, matrix products, local(): jnp.einsum('hrk,khd->hrd', raw_weights.astype(jnp.bfloat16), value_heads,...  11.8 us
    all_gather x1, waiting for transfers between devices, local(): lax.all_gather(finished_keys, ('slab', 'seq'), axis=0, tiled=True)  10.7 us
  transfers between devices with their start and end apart: 6, of which 5 were waited for; matrix products, arithmetic and copies ran while one was open for 16% of the time, Pallas kernels for 0%

commit v1 on v0

--- a/solution.py
+++ b/solution.py
@@ -7,6 +7,20 @@
 HEADS = 40
 HD = 128
 EPSILON = 1e-06
+
+
+def work_both_ways(x, axis, dim, make, out_dim):
+    ways, here, step = (lax.axis_size(axis), lax.axis_index(axis), x.shape[dim])
+    earlier, later = ([], [])
+    going_up = going_down = x
+    for far in range(ways // 2 + 1):
+        earlier.append(make(going_up, (here - far) % ways * step))
+        if 0 < far < ways - ways // 2:
+            later.append(make(going_down, (here + far) % ways * step))
+        going_up = lax.ppermute(going_up, axis, [(d, (d + 1) % ways) for d in range(ways)])
+        going_down = lax.ppermute(going_down, axis, [(d, (d - 1) % ways) for d in range(ways)])
+    line = jnp.concatenate([*earlier[::-1], *later], axis=out_dim)
+    return jnp.roll(line, (here - ways // 2) * earlier[0].shape[out_dim], axis=out_dim)
 
 
 def local(
@@ -78,10 +92,15 @@
         lax.psum_scatter(row_mass * factor, "slab", scatter_dimension=1, tiled=True),
     )
     row_share = (sum_share / mass_share[:, :, None]).astype(jnp.bfloat16)
-    attended = lax.all_gather(row_share, "slab", axis=1, tiled=True)
     weight_heads = out_weight.reshape(head_count, HD, out_weight.shape[1])
-    projected = jnp.einsum(
-        "hrd,hdc->rc", attended, weight_heads, preferred_element_type=jnp.float32
+    projected = work_both_ways(
+        row_share,
+        "slab",
+        1,
+        lambda part, at: jnp.einsum(
+            "hrd,hdc->rc", part, weight_heads, preferred_element_type=jnp.float32
+        ),
+        0,
     )
     summed = lax.psum_scatter(projected, "head", scatter_dimension=1, tiled=True)
     half = time_weight.shape[0] // 2

time: 241 us -> 234 us (0.971)
  waiting for transfers between devices: 131 us -> 117 us
  starting transfers between devices: 0.2 us -> 4.53 us
  matrix products: 25.7 us -> 28.7 us
    all_gather x1 -> x0, waiting for transfers between devices: 32.2 us -> none  [local(): attended = lax.all_gather(row_share, 'slab', axis=1, tiled=True)]
    ppermute x0 -> x3, waiting for transfers between devices: none -> 19.3 us  [the longest x2 19.3 us: work_both_ways(): lax.ppermute(going_up, axis, [(d, (d + 1) % ways) for d in range(ways)])]
    ppermute x0 -> x3, starting transfers between devices: none -> 4.36 us  [the longest x1 3.82 us: work_both_ways(): lax.ppermute(going_down, axis, [(d, (d - 1) % ways) for d in range(ways)])]
    dot_general x1 -> x4, matrix products: 6.19 us -> 9.12 us  [local(): jnp.einsum('hrd,hdc->rc', part, weight_heads, preferred_element_type=jnp....]
    unnamed x7 -> x6, waiting for transfers between devices: 15.2 us -> 15 us
    unnamed x19 -> x26, local copies, waits for them, and re-layouts: 12.4 us -> 12.5 us
  transfers between devices with their start and end apart: 6 -> 8, of which waited for: 5 -> 6; matrix products, arithmetic and copies ran while one was open for 16% -> 20% of each run, Pallas kernels for 0% -> 0%
where the time goes in v1:
time: 234 us
  waiting for transfers between devices  117 us (50%)
  blocking collectives  29.2 us (12%)
  matrix products  28.7 us (12%)
  local copies, waits for them, and re-layouts  24.8 us (11%)
  between operations  14.7 us (6%)
  other arithmetic  14.5 us (6%)
  starting transfers between devices  4.53 us (2%)
    reduce_scatter x1, waiting for transfers between devices, local(): lax.psum_scatter(partial_value * factor[:, :, None], 'slab', scatter_dime...  51.8 us
    reduce_scatter x1, waiting for transfers between devices, local(): lax.psum_scatter(projected, 'head', scatter_dimension=1, tiled=True)  20.4 us
    ppermute x2, waiting for transfers between devices, work_both_ways(): lax.ppermute(going_up, axis, [(d, (d + 1) % ways) for d in range(ways)])  19.3 us
    pmax x1, blocking collectives, local(): global_top = lax.pmax(row_top, 'slab')  18.7 us
    unnamed x6, waiting for transfers between devices  15 us
    unnamed x26, local copies, waits for them, and re-layouts  12.5 us
    dot_general x2, matrix products, local(): jnp.einsum('hrk,khd->hrd', raw_weights.astype(jnp.bfloat16), value_heads,...  11.9 us
    all_gather x1, waiting for transfers between devices, local(): lax.all_gather(finished_keys, ('slab', 'seq'), axis=0, tiled=True)  10.7 us
  transfers between devices with their start and end apart: 8, of which 6 were waited for; matrix products, arithmetic and copies ran while one was open for 20% of the time, Pallas kernels for 0%

profile of v1, /device:TPU:0, one launch (start us, length us, event | category | flops | bytes accessed | tf_op | source)
XLA Modules:
  0.0 233.6 jit_solution(7393033937256761838)
XLA Ops:
  8.1 4.6 %copy.41 = bf16[512,2560]{0,1:T(8,128)(2,1)} copy(bf16[512,2560]{1,0:T(8,128)(2,1)} %param.15) | data formatting | bytes 5242880 | tf_op args[3]
  14.0 4.5 %copy.34 = bf16[512,2560]{0,1:T(8,128)(2,1)} copy(bf16[512,2560]{1,0:T(8,128)(2,1)} %param.14) | data formatting | bytes 5242880 | tf_op args[2]
  18.4 2.7 %all_gather.13 = bf16[128,2560]{1,0:T(8,128)(2,1)S(1)} all-gather(bf16[64,2560]{1,0:T(8,128)(2,1)S(1)} %copy-done.4), channel_id=1, replica_groups=mesh['grp'=2,'slab'=4,'head'=2,'seq'=2] {'seq'}, dimensions={0}, use_global_device_ids=true | all-gather | bytes 983040 | tf_op jit(solution)/shard_map/all_gather | solution.py:56
  22.2 2.3 all_gather.15
  25.9 5.5 %psum.7 = f32[256]{0:T(256)S(1)} all-reduce(f32[256]{0:T(256)S(1)} %fusion.6), channel_id=1, replica_groups=mesh['grp'=2,'slab'=4,'head'=2,'seq'=2] {'head'}, use_global_device_ids=true, to_apply=%region_1.0 | all-reduce | flops 256 | bytes 2048 | tf_op jit(solution)/shard_map/psum | solution.py:43
  34.7 10.7 %all-gather.3.cloned.1.call-done = bf16[512,2560]{1,0:T(8,128)(2,1)} async-done(((bf16[64,2560]{1,0:T(8,128)(2,1)}), bf16[512,2560]{1,0:T(8,128)(2,1)}) %all-gather.3.cloned.1.call-update) | async-done | bytes 2621456 | tf_op jit(solution)/shard_map/all_gather | solution.py:52
  45.4 4.4 %copy.33 = bf16[512,2560]{0,1:T(8,128)(2,1)} copy(bf16[512,2560]{1,0:T(8,128)(2,1)} %all-gather.3.cloned.1.call-done) | data formatting | bytes 5242880 | tf_op jit(solution)/shard_map/all_gather | solution.py:52
  49.8 2.1 broadcast_select_fusion.1
  52.0 5.7 %multiply_reduce_fusion = (f32[20,256]{1,0:T(8,128)S(1)}, f32[20,256,512]{2,1,0:T(8,128)}) fusion(bf16[256,20,128]{0,2,1:T(8,128)(2,1)S(1)} %bitcast.43, bf16[512,20,128]{0,2,1:T(8,128)(2,1)S(1)} %bitcast.45), kind=kOutput, calls=%fused_computation.1 | convolution fusion | flops 676326400 | bytes 14438400 | tf_op jit(solution)/shard_map/rhd,khd->hrk/dot_general | solution.py:69
  57.6 18.7 %pmax.7 = f32[20,256]{1,0:T(8,128)S(1)} all-reduce(f32[20,256]{1,0:T(8,128)S(1)} %max.9), channel_id=1, replica_groups=mesh['grp'=2,'slab'=4,'head'=2,'seq'=2] {'slab'}, use_global_device_ids=true, to_apply=%region_4.5 | all-reduce | flops 5120 | bytes 40960 | tf_op jit(solution)/shard_map/pmax | solution.py:86
  76.4 5.9 %fusion = f32[20,256]{1,0:T(8,128)S(1)} fusion(f32[20,256,512]{2,1,0:T(8,128)} %get-tuple-element.8, f32[20,256]{1,0:T(8,128)S(1)} %max.9), kind=kLoop, calls=%fused_computation.2 | loop fusion | flops 7859200 | bytes 10526720 | tf_op jit(solution)/shard_map/reduce_sum | solution.py:78
  82.3 4.5 %copy.40 = bf16[512,2560]{0,1:T(8,128)(2,1)} copy(bf16[512,2560]{1,0:T(8,128)(2,1)} %all-gather.5.cloned.1.call-done) | data formatting | bytes 5242880 | tf_op jit(solution)/shard_map/all_gather | solution.py:53
  86.7 2.0 broadcast_select_fusion
  88.7 7.7 %fusion.2 = f32[20,256,128]{2,1,0:T(8,128)} fusion(bf16[512,20,128]{0,2,1:T(8,128)(2,1)S(1)} %bitcast.44, f32[20,256,512]{2,1,0:T(8,128)} %get-tuple-element.8, f32[20,256]{1,0:T(8,128)S(1)} %max.9), kind=kOutput, calls=%fused_computation.4 | convolution fusion | flops 678952960 | bytes 15749120 | tf_op jit(solution)/shard_map/hrk,khd->hrd/dot_general | solution.py:80
  97.8 4.2 %add_multiply_fusion = f32[20,256,128]{2,1,0:T(8,128)} fusion(f32[20,256,128]{2,1,0:T(8,128)} %fusion.2, bf16[128,20,128]{0,2,1:T(8,128)(2,1)} %bitcast.46, f32[20,256,128]{1,2,0:T(8,128)S(1)} %get-tuple-element.10, f32[20,256]{1,0:T(8,128)S(1)} %get-tuple-element.6, f32[20,256]{1,0:T(8,128)S(1)} %max.9), kind=kOutput, calls=%fused_computation.12 | convolution fusion | flops 171048960 | bytes 8560640 | tf_op jit(solution)/shard_map/hrk,khd->hrd/dot_general | solution.py:80
  102.0 13.5 %reduce-scatter.10.cloned.1.call-done = f32[64,20]{1,0:T(8,128)} async-done(((f32[256,20]{1,0:T(8,128)}), f32[64,20]{1,0:T(8,128)}) %reduce-scatter.10.cloned.1.call-update) | async-done | bytes 5136
  116.4 51.8 %reduce-scatter.6.cloned.1.call-done = f32[20,64,128]{2,1,0:T(8,128)} async-done(((f32[20,256,128]{2,1,0:T(8,128)}), f32[20,64,128]{2,1,0:T(8,128)}) %reduce-scatter.6.cloned.1.call-update) | async-done | bytes 655376 | tf_op jit(solution)/shard_map/reduce_scatter | solution.py:89
  170.1 10.5 %collective-permute-done = bf16[20,64,128]{2,1,0:T(8,128)(2,1)} collective-permute-done((bf16[20,64,128]{2,1,0:T(8,128)(2,1)S(1)}, bf16[20,64,128]{2,1,0:T(8,128)(2,1)}, u32[]{:S(2)}, u32[]{:S(2)}) %collective-permute-start) | collective-permute-done | bytes 327712 | tf_op jit(solution)/shard_map/ppermute | solution.py:20
  180.5 3.8 %collective-permute-start.2 = (bf16[20,64,128]{2,1,0:T(8,128)(2,1)S(1)}, bf16[20,64,128]{2,1,0:T(8,128)(2,1)S(1)}, u32[]{:S(2)}, u32[]{:S(2)}) collective-permute-start(bf16[20,64,128]{2,1,0:T(8,128)(2,1)S(1)} %divide_convert_fusion), channel_id=1, source_target_pairs={{0,12},{4,0},{8,4},{12,8},{1,13},{5,1},{9,5},{13,9},{2,14},{6,2},{... | collective-permute-start | bytes 983048 | tf_op jit(solution)/shard_map/ppermute | solution.py:21
  184.3 8.9 %collective-permute-done.1 = bf16[20,64,128]{2,1,0:T(8,128)(2,1)} collective-permute-done((bf16[20,64,128]{2,1,0:T(8,128)(2,1)}, bf16[20,64,128]{2,1,0:T(8,128)(2,1)}, u32[]{:S(2)}, u32[]{:S(2)}) %collective-permute-start.1) | collective-permute-done | bytes 327712 | tf_op jit(solution)/shard_map/ppermute | solution.py:20
  193.2 4.4 %constant_dynamic-update-slice_fusion.7 = (f32[512,1280]{1,0:T(8,128)S(1)}, f32[64,1280]{1,0:T(8,128)S(1)}) fusion(bf16[20,64,128]{2,1,0:T(8,128)(2,1)} %collective-permute-done.1, bf16[20,128,1280]{2,1,0:T(8,128)(2,1)} %bitcast.36), kind=kOutput, calls=%fused_computation.37 | convolution fusion | flops 419430400 | bytes 7536640 | tf_op jit(solution)/shard_map/hrd,hdc->rc/dot_general | solution.py:100
  197.6 2.2 constant_dynamic-update-slice_fusion.6
  204.9 20.4 %reduce-scatter.8.cloned.1.call-done = f32[256,640]{1,0:T(8,128)} async-done(((f32[256,1280]{1,0:T(8,128)}), f32[256,640]{1,0:T(8,128)}) %reduce-scatter.8.cloned.1.call-update) | async-done | bytes 655376 | tf_op jit(solution)/shard_map/reduce_scatter | solution.py:105
  225.2 1.9 multiply_convert_fusion
  (57 shorter events, 16.3 us)
Async XLA Ops:
  6.5 197.9 %copy-start = (f32[256,640]{1,0:T(8,128)S(1)}, f32[256,640]{1,0:T(8,128)}, u32[]{:S(2)}) copy-start(f32[256,640]{1,0:T(8,128)} %param.21) | copy-start | bytes 1966084
  6.5 38.9 %all-gather.3.cloned.1.call-start = ((), (), s32[]{:S(2)}) async-start(), calls=%async_computation.3 | async-start | bytes 2949120 | tf_op jit(solution)/shard_map/all_gather | solution.py:52
  7.3 75.0 %all-gather.5.cloned.1.call-start = ((), (), s32[]{:S(2)}) async-start(), calls=%async_computation.4 | async-start | bytes 2949120 | tf_op jit(solution)/shard_map/all_gather | solution.py:53
  8.0 107.5 %reduce-scatter.10.cloned.1.call-start = ((), (), s32[]{:S(2)}) async-start(), calls=%async_computation.7 | async-start | bytes 163840
  8.1 5.2 %copy-start.3 = (bf16[256,2560]{1,0:T(8,128)(2,1)S(1)}, bf16[256,2560]{1,0:T(8,128)(2,1)}, u32[]{:S(2)}) copy-start(bf16[256,2560]{1,0:T(8,128)(2,1)} %param.12) | copy-start | bytes 3932164
  13.9 4.5 %copy-start.4 = (bf16[64,2560]{1,0:T(8,128)(2,1)S(1)}, bf16[64,2560]{1,0:T(8,128)(2,1)}, u32[]{:S(2)}) copy-start(bf16[64,2560]{1,0:T(8,128)(2,1)} %param.18) | copy-start | bytes 983044
  13.9 8.3 %copy-start.5 = (bf16[64,2560]{1,0:T(8,128)(2,1)S(1)}, bf16[64,2560]{1,0:T(8,128)(2,1)}, u32[]{:S(2)}) copy-start(bf16[64,2560]{1,0:T(8,128)(2,1)} %param.19) | copy-start | bytes 983044
  21.1 10.4 %copy-start.6 = (f32[2560]{0:T(1024)S(1)}, f32[2560]{0:T(1024)}, u32[]{:S(2)}) copy-start(f32[2560]{0:T(1024)} %param.13) | copy-start | bytes 30724
  31.9 1.2 copy-start.1
  49.8 2.1 copy-start.2
  97.7 70.5 %reduce-scatter.6.cloned.1.call-start = ((), (), s32[]{:S(2)}) async-start(), calls=%async_computation.5 | async-start | bytes 3276800 | tf_op jit(solution)/shard_map/reduce_scatter | solution.py:89
  101.9 95.6 %slice-start = ((s8[6553600]{0:T(1024)(128)(4,1)}), s8[2359296]{0:T(1024)(128)(4,1)S(1)}, s32[]{:S(2)}) async-start(s8[6553600]{0:T(1024)(128)(4,1)} %bitcast.37), calls=%async_computation.8 | async-start | bytes 4718592
  102.0 123.3 %reduce-scatter.8.cloned.1.call-start = ((), (), s32[]{:S(2)}) async-start(), calls=%async_computation.6 | async-start | bytes 1966080 | tf_op jit(solution)/shard_map/reduce_scatter | solution.py:105
  169.5 11.0 %collective-permute-start = (bf16[20,64,128]{2,1,0:T(8,128)(2,1)S(1)}, bf16[20,64,128]{2,1,0:T(8,128)(2,1)}, u32[]{:S(2)}, u32[]{:S(2)}) collective-permute-start(bf16[20,64,128]{2,1,0:T(8,128)(2,1)S(1)} %divide_convert_fusion), channel_id=1, source_target_pairs={{0,4},{4,8},{8,12},{12,0},{1,5},{5,9},{9,13},{13,1},{2,6},{6,10},{... | collective-permute-start | bytes 983048 | tf_op jit(solution)/shard_map/ppermute | solution.py:20
  180.5 12.7 %collective-permute-start.1 = (bf16[20,64,128]{2,1,0:T(8,128)(2,1)}, bf16[20,64,128]{2,1,0:T(8,128)(2,1)}, u32[]{:S(2)}, u32[]{:S(2)}) collective-permute-start(bf16[20,64,128]{2,1,0:T(8,128)(2,1)} %collective-permute-done), channel_id=1, source_target_pairs={{0,4},{4,8},{8,12},{12,0},{1,5},{5,9},{9,13},{13,1},{2,6},{6,10},{... | collective-permute-start | bytes 983048 | tf_op jit(solution)/shard_map/ppermute | solution.py:20
  180.5 20.6 %collective-permute-start.2 = (bf16[20,64,128]{2,1,0:T(8,128)(2,1)S(1)}, bf16[20,64,128]{2,1,0:T(8,128)(2,1)S(1)}, u32[]{:S(2)}, u32[]{:S(2)}) collective-permute-start(bf16[20,64,128]{2,1,0:T(8,128)(2,1)S(1)} %divide_convert_fusion), channel_id=1, source_target_pairs={{0,12},{4,0},{8,4},{12,8},{1,13},{5,1},{9,5},{13,9},{2,14},{6,2},{... | collective-permute-start | bytes 983048 | tf_op jit(solution)/shard_map/ppermute | solution.py:21
  193.2 4.4 %slice-start.1 = ((s8[6553600]{0:T(1024)(128)(4,1)}), s8[4194304]{0:T(1024)(128)(4,1)S(1)}, s32[]{:S(2)}) async-start(s8[6553600]{0:T(1024)(128)(4,1)} %bitcast.37), calls=%async_computation.9 | async-start | bytes 8388608
Sparse Core Ops, SparseCore 0:
  9.0 36.4 all-gather.2
  47.1 33.8 all-gather.4
  97.8 17.6 reduce-scatter.9
  117.7 50.4 reduce-scatter.5
  203.8 21.3 reduce-scatter.7
